TPU v7x, 32 devices: a whole 2x2x4 slice. The times are simulated.
32 devices in a mesh: group: 4 (over x, core), dev: 8 (over z, y).
Axes of the slice: x: 2, y: 2, z: 4, core: 2. Of those that a mesh axis runs over, the one named last changes fastest.
Arguments:
- adjoint_seed: bfloat16 [64, 3, 48, 16, 128], P(('group', 'dev')), may hold values from -6 to 6
- stiffness: float32 [64, 48, 16, 128], P(('group', 'dev')), may hold values from 0.1 to 0.4
- lengths: int32 [64], P(('group', 'dev')), may hold values from 24 to 48, as said below
- conn_lower: int32 [64, 3], P(('group', 'dev')), may hold values from -1 to 7, as said below
- conn_upper: int32 [64, 3], P(('group', 'dev')), may hold values from -1 to 7, as said below
- coord_x: float32 [64, 48], P(('group', 'dev')), may hold values from 0 to 95
- coord_y: float32 [64, 16], P(('group', 'dev')), may hold values from 0 to 63
- coord_z: float32 [64, 128], P(('group', 'dev')), may hold values from 0 to 31
Outputs:
- adjoint_field: float32 [64, 3, 48, 16, 128], P(('group', 'dev'))
- lattice_grad: float32 [96, 6144], P('dev')
Inputs may be any that keep to these rules, and one draw needn't show every extreme that they name: `conn_lower`: each row names, within the same cluster of 16 blocks, the device index along dev and the slot of the block whose upper face meets this block's lower face (first entry -1 for a wall, then 0 and 0), and 1 in the third entry where that face is reversed along the second grid dimension. A cluster's links form one chain through all its blocks; each link appears mirrored in conn_upper with the same orientation. `conn_upper`: likewise for the block across the upper face, whose lower face it meets. `lengths`: in every cluster some block has 48 active rows and some 48 // 2.
All inputs are finite; a program needn't handle non-finite values.
Results may differ from a plain program's by a relative error of at most 0.0003.
Values sent between devices are 32-bit elements; how exact they have to be, the bound alone decides.
No kernel may reach another device: no remote copies, remote signals or barrier semaphores. Data moves between devices by JAX's collectives and lax.ppermute only.
A program may use at most 64 MiB of HBM per device.

v0:
```python
import math
import jax
import jax.numpy as jnp
from jax import lax
from jax.sharding import PartitionSpec as P

CX = 48
CY = 16
CZ = 128
LX = 96
LY = 64
LZ = 32
SWEEPS = 2
TAPS = [
    (shift_x, shift_y, shift_z, 1.0 / (shift_x * shift_x + shift_y * shift_y + shift_z * shift_z))
    for shift_x in (-1, 0, 1)
    for shift_y in (-1, 0, 1)
    for shift_z in (-1, 0, 1)
    if (shift_x, shift_y, shift_z) != (0, 0, 0)
]
DOMINANCE = 1.25


def stencil(padded, count_x, count_y, count_z):
    running = None
    for shift_x, shift_y, shift_z, factor in TAPS:
        window = padded[
            :,
            1 + shift_x : 1 + shift_x + count_x,
            1 + shift_y : 1 + shift_y + count_y,
            1 + shift_z : 1 + shift_z + count_z,
        ]
        running = factor * window if running is None else running + factor * window
    return running


def extend(values, lower_halo, upper_halo, length):
    zero_row = jnp.zeros_like(lower_halo)[:, None]
    joined = jnp.concatenate([lower_halo[:, None], values, zero_row], axis=1)
    joined = lax.dynamic_update_slice(
        joined, upper_halo[:, None], (jnp.int32(0), length + 1, jnp.int32(0), jnp.int32(0))
    )
    return jnp.pad(joined, ((0, 0), (0, 0), (1, 1), (1, 1)))


def end_faces(values, lengths):
    lower_face = values[:, :, 0]
    upper_face = jax.vmap(
        lambda block_values, length: lax.dynamic_index_in_dim(
            block_values, length - 1, axis=1, keepdims=False
        )
    )(values, lengths)
    return jnp.stack([lower_face, upper_face], axis=1)


def partner_tiles(face_tiles, links, side, slots):
    partner = jnp.maximum(links[:, 0], 0) * slots + links[:, 1]
    chosen = face_tiles[partner, side]
    mirrored = chosen[..., ::-1, :]
    turned = jnp.where((links[:, 2] == 1)[:, None, None, None], mirrored, chosen)
    return jnp.where((links[:, 0] >= 0)[:, None, None, None], turned, jnp.zeros_like(turned))


def hat(coords, points):
    grid_points = jnp.arange(points, dtype=jnp.float32)[None, :, None]
    return jnp.maximum(0.0, 1.0 - jnp.abs(grid_points - coords[:, None, :]))


def on_device(adjoint_seed, stiffness, lengths, conn_lower, conn_upper, coord_x, coord_y, coord_z):
    slots = stiffness.shape[0]
    active = (jnp.arange(CX, dtype=jnp.int32)[None, :] < lengths[:, None]).astype(jnp.float32)[
        :, :, None, None
    ]
    stiff_masked = stiffness * active
    stiff_tiles = lax.all_gather(
        end_faces(stiff_masked[:, None], lengths), "dev", axis=0, tiled=True
    )
    stiff_lower = partner_tiles(stiff_tiles, conn_lower, 1, slots)
    stiff_upper = partner_tiles(stiff_tiles, conn_upper, 0, slots)

    def diagonal_one(stiff_block, lower_halo, upper_halo, length):
        near = stencil(extend(stiff_block[None], lower_halo, upper_halo, length), CX, CY, CZ)[0]
        return DOMINANCE * stiff_block * near

    diagonal = jax.vmap(diagonal_one)(stiff_masked, stiff_lower, stiff_upper, lengths)
    safe = jnp.where(active > 0, diagonal, jnp.ones_like(diagonal))
    source = adjoint_seed.astype(jnp.float32) * active[:, None]
    adjoint = source / safe[:, None]

    def sweep_one(values, low_tile, high_tile, length, stiff_block, source_block, safe_block):
        near = stencil(extend(values, low_tile, high_tile, length), CX, CY, CZ)
        return (source_block + stiff_block[None] * near) / safe_block[None]

    for sweep_index in range(SWEEPS):
        weighted = stiff_masked[:, None] * adjoint
        weighted_tiles = lax.all_gather(end_faces(weighted, lengths), "dev", axis=0, tiled=True)
        lower_halo = partner_tiles(weighted_tiles, conn_lower, 1, slots)
        upper_halo = partner_tiles(weighted_tiles, conn_upper, 0, slots)
        adjoint = jax.vmap(sweep_one)(
            weighted, lower_halo, upper_halo, lengths, stiff_masked, source, safe
        )
    hat_x = hat(coord_x, LX)
    hat_y = hat(coord_y, LY)
    hat_z = hat(coord_z, LZ)
    first = jnp.einsum("bcxyz,bnz->bcxyn", adjoint, hat_z, precision=lax.Precision.HIGHEST)
    second = jnp.einsum("bcxyn,bmy->bxcmn", first, hat_y, precision=lax.Precision.HIGHEST)
    contracted = second.reshape(slots * CX, 3 * LY * LZ)
    hat_rows = jnp.transpose(hat_x, (1, 0, 2)).reshape(LX, slots * CX)
    scale = math.sqrt(
        LX * LY * LZ / (lax.axis_size("group") * lax.axis_size("dev") * slots * CX * CY * CZ)
    )
    partial_value = lax.psum_scatter(
        jnp.dot(
            hat_rows,
            contracted,
            precision=lax.Precision.HIGHEST,
            preferred_element_type=jnp.float32,
        ),
        "dev",
        scatter_dimension=0,
        tiled=True,
    )
    owned = lax.psum(partial_value, "group")
    return (adjoint, owned * scale)


def solution(mesh):
    in_specs = (
        P(("group", "dev"), None, None, None, None),
        P(("group", "dev"), None, None, None),
        P(("group", "dev")),
        P(("group", "dev"), None),
        P(("group", "dev"), None),
        P(("group", "dev"), None),
        P(("group", "dev"), None),
        P(("group", "dev"), None),
    )
    out_specs = (P(("group", "dev"), None, None, None, None), P("dev", None))
    return jax.shard_map(
        on_device, mesh=mesh, in_specs=in_specs, out_specs=out_specs, check_vma=False
    )
```

profile of v0, /device:TPU:0, one launch (start us, length us, event | category | flops | bytes accessed | tf_op | source)
XLA Modules:
  0.0 348.4 jit_solution(1823001275424142487)
XLA Ops:
  7.3 0.7 broadcast_compare_fusion
  8.0 0.7 fusion.188
  8.6 1.3 fusion.204
  11.1 32.6 %all_gather.9 = f32[16,2,1,16,128]{4,3,0,2,1:T(8,128)S(1)} all-gather(f32[2,2,1,16,128]{4,3,0,2,1:T(8,128)S(1)} %pad_maximum_fusion.2), channel_id=1, replica_groups=mesh['group'=4,'dev'=8] {'dev'}, dimensions={0}, use_global_device_ids=true | all-gather | bytes 294912 | tf_op jit(solution)/shard_map/all_gather | solution.py:75
  46.1 15.4 %while.3 = (s32[]{:T(128)}, f32[2,1,50,16,128]{4,3,0,2,1:T(8,128)S(1)}, s32[2,5]{1,0:T(2,128)S(1)}, f32[2,1,1,16,128]{4,3,2,1,0:T(8,128)S(1)}, s32[]{:T(128)}, /*index=5*/s32[5]{0:T(128)S(1)}) while((s32[]{:T(128)}, f32[2,1,50,16,128]{4,3,0,2,1:T(8,128)S(1)}, s32[2,5]{1,0:T(2,128)S(1)}, f32[2,1,1,16,128]{4,3,2,1,0:T(8,128)S(1)}, s32[]{:T(128)}, ...), condition=%wide.while_cond, body=%wide.while_body.sunk | while | flops 2069 | bytes 41215 | solution.py:40
  46.2 0.7 fusion.208
  46.8 3.2 concatenate.70
  50.0 0.7 and_reduce_fusion.6
  50.7 1.3 constant_dynamic-slice_fusion.14
  51.9 1.9 bitcast_dynamic-update-slice_fusion.6
  53.9 0.7 fusion.208
  54.5 3.2 concatenate.70
  57.7 0.7 and_reduce_fusion.6
  58.4 1.3 constant_dynamic-slice_fusion.14
  59.7 1.9 bitcast_dynamic-update-slice_fusion.6
  61.6 4.2 %fusion.142 = f32[2,48,16,128]{3,2,0,1:T(8,128)S(1)} fusion(f32[2,1,50,16,128]{4,3,0,2,1:T(8,128)S(1)} %get-tuple-element.7, pred[2,48]{0,1:T(8,128)(4,1)S(1)} %get-tuple-element.113, f32[2,48]{0,1:T(8,128)S(1)} %get-tuple-element.114, f32[2,48,16,128]{3,2,1,0:T(8,128)S(1)} %copy-done.4), kind=kLoop, calls=%fused_computation.243 | loop fusion | flops 9633792 | bytes 3995648 | tf_op jit(solution)/shard_map/jit(_where)/select_n | solution.py:86
  65.7 1.9 divide_multiply_fusion
  67.7 1.7 copy.85
  69.9 2.2 gather_fusion.7
  72.1 31.7 %all_gather.10 = f32[16,2,3,16,128]{4,3,2,0,1:T(8,128)S(1)} all-gather(f32[2,2,3,16,128]{4,3,2,0,1:T(8,128)S(1)} %pad_maximum_fusion), channel_id=1, replica_groups=mesh['group'=4,'dev'=8] {'dev'}, dimensions={0}, use_global_device_ids=true | all-gather | bytes 884736 | tf_op jit(solution)/shard_map/all_gather | solution.py:96
  105.2 1.9 maximum_maximum_fusion
  107.1 15.0 %while.4 = (s32[]{:T(128)}, f32[2,3,50,16,128]{4,3,1,0,2:T(8,128)S(1)}, s32[2,5]{1,0:T(2,128)S(1)}, f32[2,3,1,16,128]{4,3,2,1,0:T(8,128)S(1)}, s32[]{:T(128)}, /*index=5*/s32[5]{0:T(128)S(1)}) while((s32[]{:T(128)}, f32[2,3,50,16,128]{4,3,1,0,2:T(8,128)S(1)}, s32[2,5]{1,0:T(2,128)S(1)}, f32[2,3,1,16,128]{4,3,2,1,0:T(8,128)S(1)}, s32[]{:T(128)}, ...), condition=%wide.while_cond.1, body=%wide.while_body.1.sunk | while | flops 6165 | bytes 123135 | solution.py:40
  107.1 0.7 fusion.209
  107.8 3.2 concatenate.71
  110.9 0.6 and_reduce_fusion.7
  111.6 1.2 constant_dynamic-slice_fusion.16
  112.7 1.8 bitcast_dynamic-update-slice_fusion.7
  114.6 0.7 fusion.209
  115.2 3.2 concatenate.71
  118.4 0.6 and_reduce_fusion.7
  119.0 1.2 constant_dynamic-slice_fusion.16
  120.2 1.8 bitcast_dynamic-update-slice_fusion.7
  122.1 13.0 %fusion.97 = f32[2,3,48,16,128]{4,3,1,0,2:T(8,128)S(1)} fusion(f32[2,3,50,16,128]{4,3,1,0,2:T(8,128)S(1)} %get-tuple-element.15, f32[2,48,16,128]{3,2,0,1:T(8,128)} %copy-done.2, f32[2,48,16,128]{3,2,0,1:T(8,128)S(1)} %copy_multiply_fusion, f32[2,48]{0,1:T(8,128)S(1)} %get-tuple-element.114, bf16[2,3,48,16,128]{4,3,2,1,0:T(8,128)(2,1)} %param.8), kind=kLoop, calls=%fused_computation.196 | loop fusion | flops 30081024 | bytes 12312576 | tf_op jit(solution)/shard_map/mul | solution.py:95
  135.2 1.2 copy-done.1
  137.0 32.2 %all_gather.11 = f32[16,2,3,16,128]{4,3,2,0,1:T(8,128)S(1)} all-gather(f32[2,2,3,16,128]{4,3,2,0,1:T(8,128)S(1)} %pad_maximum_fusion.1), channel_id=1, replica_groups=mesh['group'=4,'dev'=8] {'dev'}, dimensions={0}, use_global_device_ids=true | all-gather | bytes 884736 | tf_op jit(solution)/shard_map/all_gather | solution.py:96
  170.5 1.9 maximum_maximum_fusion.1
  172.4 15.0 %while.5 = (s32[]{:T(128)}, f32[2,3,50,16,128]{4,3,1,0,2:T(8,128)S(1)}, s32[2,5]{1,0:T(2,128)S(1)}, f32[2,3,1,16,128]{4,3,2,1,0:T(8,128)S(1)}, s32[]{:T(128)}, /*index=5*/s32[5]{0:T(128)S(1)}) while((s32[]{:T(128)}, f32[2,3,50,16,128]{4,3,1,0,2:T(8,128)S(1)}, s32[2,5]{1,0:T(2,128)S(1)}, f32[2,3,1,16,128]{4,3,2,1,0:T(8,128)S(1)}, s32[]{:T(128)}, ...), condition=%wide.while_cond.2, body=%wide.while_body.2.sunk | while | flops 6165 | bytes 123135 | solution.py:40
  172.5 0.7 fusion.210
  173.1 3.2 concatenate.72
  176.3 0.6 and_reduce_fusion.8
  176.9 1.2 constant_dynamic-slice_fusion.18
  178.1 1.8 bitcast_dynamic-update-slice_fusion.8
  179.9 0.7 fusion.210
  180.6 3.2 concatenate.72
  183.8 0.6 and_reduce_fusion.8
  184.4 1.2 constant_dynamic-slice_fusion.18
  185.6 1.8 bitcast_dynamic-update-slice_fusion.8
  187.4 13.0 %fusion.93 = f32[2,3,48,16,128]{4,3,1,0,2:T(8,128)S(1)} fusion(f32[2,3,50,16,128]{4,3,1,0,2:T(8,128)S(1)} %get-tuple-element.23, f32[2,48,16,128]{3,2,0,1:T(8,128)} %copy-done.2, f32[2,48,16,128]{3,2,0,1:T(8,128)S(1)} %copy_multiply_fusion, f32[2,48]{0,1:T(8,128)S(1)} %get-tuple-element.114, bf16[2,3,48,16,128]{4,3,2,1,0:T(8,128)(2,1)} %param.8), kind=kLoop, calls=%fused_computation.190 | loop fusion | flops 29491200 | bytes 12312576 | tf_op jit(solution)/shard_map/vmap()/div | solution.py:92
  200.7 1.4 copy-done.3
  202.1 2.1 fusion.152
  204.2 2.3 copy.98
  206.5 10.4 %convolution_bitcast_fusion = f32[2,48,3,64,32]{3,1,4,2,0:T(8,128)} fusion(f32[2,3,48,16,32]{2,3,4,1,0:T(8,128)} %copy.98, f32[2,16]{1,0:T(2,128)S(1)} %copy-done.5), kind=kOutput, calls=%fused_computation.197 | convolution fusion | flops 113254400 | bytes 2949248 | tf_op jit(solution)/shard_map/bcxyn,bmy->bxcmn/dot_general | solution.py:106
  216.9 9.6 %copy.99 = f32[2,48,3,64,32]{1,0,4,3,2:T(2,128)} copy(f32[2,48,3,64,32]{3,1,4,2,0:T(8,128)} %convolution_bitcast_fusion) | data formatting | bytes 4718592 | tf_op jit(solution)/shard_map/bcxyn,bmy->bxcmn/transpose | solution.py:106
  226.5 6.1 %reshape.97 = f32[96,6144]{0,1:T(8,128)S(1)} reshape(f32[2,48,3,64,32]{1,0,4,3,2:T(2,128)} %copy.99) | data formatting | bytes 4718592 | tf_op jit(solution)/shard_map/reshape | solution.py:107
  232.6 4.7 %fusion.146 = f32[96,6144]{1,0:T(8,128)} fusion(f32[96,6144]{0,1:T(8,128)S(1)} %reshape.97, f32[96]{0:T(128)S(1)} %sub.71), kind=kOutput, calls=%fused_computation.253 | convolution fusion | flops 679514112 | bytes 4718976 | tf_op jit(solution)/shard_map/dot_general | solution.py:113
  237.3 50.6 %fusion = f32[16,6144]{1,0:T(8,128)S(1)} fusion(f32[96,6144]{1,0:T(8,128)} %fusion.146), kind=kCustom, calls=%all-reduce-scatter | all-reduce-scatter fusion | flops 786433 | bytes 2753024
  287.9 4.4 %collective-permute-start = (f32[16,6144]{1,0:T(8,128)S(1)}, f32[16,6144]{1,0:T(8,128)S(1)}, u32[]{:S(2)}, u32[]{:S(2)}) collective-permute-start(f32[16,6144]{1,0:T(8,128)S(1)} %fusion), channel_id=1, source_target_pairs={{0,1},{1,2},{2,3},{3,4},{4,5},{5,6},{6,7},{8,9},{9,10},{10,11},{11... | collective-permute-start | bytes 1179656
  292.4 6.3 %collective-permute-start.1 = (f32[12,6144]{1,0:T(8,128)S(1)}, f32[12,6144]{1,0:T(8,128)S(1)}, u32[]{:S(2)}, u32[]{:S(2)}) collective-permute-start(f32[12,6144]{1,0:T(8,128)S(1)} %slice.489), channel_id=1, source_target_pairs={{0,2},{1,3},{2,4},{3,5},{4,6},{5,7},{8,10},{9,11},{10,12},{11,13},... | collective-permute-start | bytes 884744
  298.7 0.6 dynamic-slice.22
  300.0 4.0 %collective-permute-done.1 = f32[12,6144]{1,0:T(8,128)S(1)} collective-permute-done((f32[12,6144]{1,0:T(8,128)S(1)}, f32[12,6144]{1,0:T(8,128)S(1)}, u32[]{:S(2)}, u32[]{:S(2)}) %collective-permute-start.1) | collective-permute-done | bytes 294944
  304.0 1.0 concatenate.66
  305.0 0.8 constant_dynamic-slice_fusion.6
  305.8 33.9 %all-reduce.9.cloned.1.call-done = f32[12,6144]{1,0:T(8,128)} async-done(((f32[12,6144]{1,0:T(8,128)}), f32[12,6144]{1,0:T(8,128)}) %all-reduce.9.cloned.1.call-update) | async-done | bytes 294928 | tf_op jit(solution)/shard_map/psum | solution.py:123
  339.8 1.8 broadcast_multiply_fusion
  (91 shorter events, 7.7 us)
Async XLA Ops:
  7.2 3.2 copy-start.9
  7.2 3.2 copy-start.4
  7.2 2.9 copy-start.6
  7.2 3.0 copy-start.7
  7.2 332.6 %all-reduce.9.cloned.1.call-start = ((), (), s32[]{:S(2)}) async-start(), calls=%async_computation | async-start | bytes 786432 | tf_op jit(solution)/shard_map/psum | solution.py:123
  9.9 36.0 %copy-start.11 = (s32[4]{0:T(128)S(1)}, s32[4]{0:T(128)}, u32[]{:S(2)}) copy-start(s32[4]{0:T(128)} %constant.25.clone.1) | copy-start | bytes 52
  10.0 36.1 %copy-start.13 = (s32[5]{0:T(128)S(1)}, s32[5]{0:T(128)}, u32[]{:S(2)}) copy-start(s32[5]{0:T(128)} %constant.656) | copy-start | bytes 64
  65.7 2.0 copy-start.2
  67.7 2.2 copy-start
  135.0 1.4 copy-start.1
  200.4 1.6 copy-start.8
  200.7 1.4 copy-start.3
  204.1 2.3 copy-start.5
  226.5 6.1 %copy-start.12 = (f32[2,48]{1,0:T(2,128)S(1)}, f32[2,48]{1,0:T(2,128)}, u32[]{:S(2)}) copy-start(f32[2,48]{1,0:T(2,128)} %param.13) | copy-start | bytes 1156
  237.3 61.4 %copy-start.10 = (u32[32]{0:T(128)S(1)}, u32[32]{0:T(128)}, u32[]{:S(2)}) copy-start(u32[32]{0:T(128)} %constant.342) | copy-start | bytes 388
  287.9 16.0 %collective-permute-start = (f32[16,6144]{1,0:T(8,128)S(1)}, f32[16,6144]{1,0:T(8,128)S(1)}, u32[]{:S(2)}, u32[]{:S(2)}) collective-permute-start(f32[16,6144]{1,0:T(8,128)S(1)} %fusion), channel_id=1, source_target_pairs={{0,1},{1,2},{2,3},{3,4},{4,5},{5,6},{6,7},{8,9},{9,10},{10,11},{11... | collective-permute-start | bytes 1179656
  292.4 11.6 %collective-permute-start.1 = (f32[12,6144]{1,0:T(8,128)S(1)}, f32[12,6144]{1,0:T(8,128)S(1)}, u32[]{:S(2)}, u32[]{:S(2)}) collective-permute-start(f32[12,6144]{1,0:T(8,128)S(1)} %slice.489), channel_id=1, source_target_pairs={{0,2},{1,3},{2,4},{3,5},{4,6},{5,7},{8,10},{9,11},{10,12},{11,13},... | collective-permute-start | bytes 884744
Sparse Core Ops, SparseCore 0:
  306.0 33.7 all-reduce.8
where the time goes:
time: 350 us; the launch traced here: 348 us
  blocking collectives  147 us (42%)
  local copies, waits for them, and re-layouts  63.7 us (18%)
  other arithmetic  56.4 us (16%)
  waiting for transfers between devices  38 us (11%)
  matrix products  17.1 us (5%)
  between operations  15.1 us (4%)
  starting transfers between devices  10.8 us (3%)
    all_gather x2, blocking collectives, on_device(): lax.all_gather(end_faces(weighted, lengths), 'dev', axis=0, tiled=True)  63.9 us
    unnamed x1, blocking collectives  50.6 us
    psum x1, waiting for transfers between devices, on_device(): owned = lax.psum(partial_value, 'group')  33.9 us
    all_gather x1, blocking collectives, on_device(): lax.all_gather(end_faces(stiff_masked[:, None], lengths), 'dev', axis=0,...  32.6 us
    scatter x24, local copies, waits for them, and re-layouts  30.2 us
    scatter x12, other arithmetic  14.9 us
    mul x2, other arithmetic, on_device(): weighted = stiff_masked[:, None] * adjoint  14.9 us
    div x1, other arithmetic, sweep_one(): return (source_block + stiff_block[None] * near) / safe_block[None]  13 us
  transfers between devices with their start and end apart: 3, of which 2 were waited for; matrix products, arithmetic and copies ran while one was open for 0% of the time, Pallas kernels for 0%

commit v1 on v0

--- a/solution.py
+++ b/solution.py
@@ -120,7 +120,7 @@
         scatter_dimension=0,
         tiled=True,
     )
-    owned = lax.psum(partial_value, "group")
+    owned = jnp.sum(lax.all_gather(partial_value, "group"), axis=0)
     return (adjoint, owned * scale)
 
 

time: 350 us -> 337 us (0.963)
  waiting for transfers between devices: 38 us -> 24.8 us
    psum x1 -> x0, waiting for transfers between devices: 33.9 us -> none  [on_device(): owned = lax.psum(partial_value, 'group')]
    all_gather x0 -> x1, waiting for transfers between devices: none -> 20.8 us  [on_device(): owned = jnp.sum(lax.all_gather(partial_value, 'group'), axis=0)]
where the time goes in v1:
time: 337 us; the launch traced here: 336 us
  blocking collectives  147 us (44%)
  local copies, waits for them, and re-layouts  63.7 us (19%)
  other arithmetic  56.9 us (17%)
  waiting for transfers between devices  24.8 us (7%)
  matrix products  17.1 us (5%)
  between operations  15.1 us (4%)
  starting transfers between devices  10.8 us (3%)
    all_gather x2, blocking collectives, on_device(): lax.all_gather(end_faces(weighted, lengths), 'dev', axis=0, tiled=True)  63.9 us
    unnamed x1, blocking collectives  50.6 us
    all_gather x1, blocking collectives, on_device(): lax.all_gather(end_faces(stiff_masked[:, None], lengths), 'dev', axis=0,...  32.6 us
    scatter x24, local copies, waits for them, and re-layouts  30.2 us
    all_gather x1, waiting for transfers between devices, on_device(): owned = jnp.sum(lax.all_gather(partial_value, 'group'), axis=0)  20.8 us
    scatter x12, other arithmetic  14.9 us
    mul x2, other arithmetic, on_device(): weighted = stiff_masked[:, None] * adjoint  14.9 us
    div x1, other arithmetic, sweep_one(): return (source_block + stiff_block[None] * near) / safe_block[None]  13 us
  transfers between devices with their start and end apart: 3, of which 2 were waited for; matrix products, arithmetic and copies ran while one was open for 0% of the time, Pallas kernels for 0%

profile of v1, /device:TPU:0, one launch (start us, length us, event | category | flops | bytes accessed | tf_op | source)
XLA Modules:
  0.0 335.8 jit_solution(13834892080746963850)
XLA Ops:
  7.3 0.7 broadcast_compare_fusion
  8.0 0.7 fusion.188
  8.6 1.3 fusion.204
  11.1 32.6 %all_gather.15 = f32[16,2,1,16,128]{4,3,0,2,1:T(8,128)S(1)} all-gather(f32[2,2,1,16,128]{4,3,0,2,1:T(8,128)S(1)} %pad_maximum_fusion.2), channel_id=1, replica_groups=mesh['group'=4,'dev'=8] {'dev'}, dimensions={0}, use_global_device_ids=true | all-gather | bytes 294912 | tf_op jit(solution)/shard_map/all_gather | solution.py:75
  46.1 15.4 %while.3 = (s32[]{:T(128)}, f32[2,1,50,16,128]{4,3,0,2,1:T(8,128)S(1)}, s32[2,5]{1,0:T(2,128)S(1)}, f32[2,1,1,16,128]{4,3,2,1,0:T(8,128)S(1)}, s32[]{:T(128)}, /*index=5*/s32[5]{0:T(128)S(1)}) while((s32[]{:T(128)}, f32[2,1,50,16,128]{4,3,0,2,1:T(8,128)S(1)}, s32[2,5]{1,0:T(2,128)S(1)}, f32[2,1,1,16,128]{4,3,2,1,0:T(8,128)S(1)}, s32[]{:T(128)}, ...), condition=%wide.while_cond, body=%wide.while_body.sunk | while | flops 2069 | bytes 41215 | solution.py:40
  46.2 0.7 fusion.208
  46.8 3.2 concatenate.70
  50.0 0.7 and_reduce_fusion.6
  50.7 1.3 constant_dynamic-slice_fusion.13
  51.9 1.9 bitcast_dynamic-update-slice_fusion.6
  53.9 0.7 fusion.208
  54.5 3.2 concatenate.70
  57.7 0.7 and_reduce_fusion.6
  58.4 1.3 constant_dynamic-slice_fusion.13
  59.7 1.9 bitcast_dynamic-update-slice_fusion.6
  61.6 4.2 %fusion.142 = f32[2,48,16,128]{3,2,0,1:T(8,128)S(1)} fusion(f32[2,1,50,16,128]{4,3,0,2,1:T(8,128)S(1)} %get-tuple-element.7, pred[2,48]{0,1:T(8,128)(4,1)S(1)} %get-tuple-element.113, f32[2,48]{0,1:T(8,128)S(1)} %get-tuple-element.114, f32[2,48,16,128]{3,2,1,0:T(8,128)S(1)} %copy-done.4), kind=kLoop, calls=%fused_computation.243 | loop fusion | flops 9633792 | bytes 3995648 | tf_op jit(solution)/shard_map/jit(_where)/select_n | solution.py:86
  65.7 1.9 divide_multiply_fusion
  67.7 1.7 copy.85
  69.9 2.2 gather_fusion.7
  72.1 31.7 %all_gather.16 = f32[16,2,3,16,128]{4,3,2,0,1:T(8,128)S(1)} all-gather(f32[2,2,3,16,128]{4,3,2,0,1:T(8,128)S(1)} %pad_maximum_fusion), channel_id=1, replica_groups=mesh['group'=4,'dev'=8] {'dev'}, dimensions={0}, use_global_device_ids=true | all-gather | bytes 884736 | tf_op jit(solution)/shard_map/all_gather | solution.py:96
  105.2 1.9 maximum_maximum_fusion
  107.1 15.0 %while.4 = (s32[]{:T(128)}, f32[2,3,50,16,128]{4,3,1,0,2:T(8,128)S(1)}, s32[2,5]{1,0:T(2,128)S(1)}, f32[2,3,1,16,128]{4,3,2,1,0:T(8,128)S(1)}, s32[]{:T(128)}, /*index=5*/s32[5]{0:T(128)S(1)}) while((s32[]{:T(128)}, f32[2,3,50,16,128]{4,3,1,0,2:T(8,128)S(1)}, s32[2,5]{1,0:T(2,128)S(1)}, f32[2,3,1,16,128]{4,3,2,1,0:T(8,128)S(1)}, s32[]{:T(128)}, ...), condition=%wide.while_cond.1, body=%wide.while_body.1.sunk | while | flops 6165 | bytes 123135 | solution.py:40
  107.1 0.7 fusion.209
  107.8 3.2 concatenate.71
  110.9 0.6 and_reduce_fusion.7
  111.6 1.2 constant_dynamic-slice_fusion.15
  112.7 1.8 bitcast_dynamic-update-slice_fusion.7
  114.6 0.7 fusion.209
  115.2 3.2 concatenate.71
  118.4 0.6 and_reduce_fusion.7
  119.0 1.2 constant_dynamic-slice_fusion.15
  120.2 1.8 bitcast_dynamic-update-slice_fusion.7
  122.1 13.0 %fusion.97 = f32[2,3,48,16,128]{4,3,1,0,2:T(8,128)S(1)} fusion(f32[2,3,50,16,128]{4,3,1,0,2:T(8,128)S(1)} %get-tuple-element.15, f32[2,48,16,128]{3,2,0,1:T(8,128)} %copy-done.2, f32[2,48,16,128]{3,2,0,1:T(8,128)S(1)} %copy_multiply_fusion, f32[2,48]{0,1:T(8,128)S(1)} %get-tuple-element.114, bf16[2,3,48,16,128]{4,3,2,1,0:T(8,128)(2,1)} %param.8), kind=kLoop, calls=%fused_computation.196 | loop fusion | flops 30081024 | bytes 12312576 | tf_op jit(solution)/shard_map/mul | solution.py:95
  135.2 1.2 copy-done.1
  137.0 32.2 %all_gather.17 = f32[16,2,3,16,128]{4,3,2,0,1:T(8,128)S(1)} all-gather(f32[2,2,3,16,128]{4,3,2,0,1:T(8,128)S(1)} %pad_maximum_fusion.1), channel_id=1, replica_groups=mesh['group'=4,'dev'=8] {'dev'}, dimensions={0}, use_global_device_ids=true | all-gather | bytes 884736 | tf_op jit(solution)/shard_map/all_gather | solution.py:96
  170.5 1.9 maximum_maximum_fusion.1
  172.4 15.0 %while.5 = (s32[]{:T(128)}, f32[2,3,50,16,128]{4,3,1,0,2:T(8,128)S(1)}, s32[2,5]{1,0:T(2,128)S(1)}, f32[2,3,1,16,128]{4,3,2,1,0:T(8,128)S(1)}, s32[]{:T(128)}, /*index=5*/s32[5]{0:T(128)S(1)}) while((s32[]{:T(128)}, f32[2,3,50,16,128]{4,3,1,0,2:T(8,128)S(1)}, s32[2,5]{1,0:T(2,128)S(1)}, f32[2,3,1,16,128]{4,3,2,1,0:T(8,128)S(1)}, s32[]{:T(128)}, ...), condition=%wide.while_cond.2, body=%wide.while_body.2.sunk | while | flops 6165 | bytes 123135 | solution.py:40
  172.5 0.7 fusion.210
  173.1 3.2 concatenate.72
  176.3 0.6 and_reduce_fusion.8
  176.9 1.2 constant_dynamic-slice_fusion.17
  178.1 1.8 bitcast_dynamic-update-slice_fusion.8
  179.9 0.7 fusion.210
  180.6 3.2 concatenate.72
  183.8 0.6 and_reduce_fusion.8
  184.4 1.2 constant_dynamic-slice_fusion.17
  185.6 1.8 bitcast_dynamic-update-slice_fusion.8
  187.4 13.0 %fusion.93 = f32[2,3,48,16,128]{4,3,1,0,2:T(8,128)S(1)} fusion(f32[2,3,50,16,128]{4,3,1,0,2:T(8,128)S(1)} %get-tuple-element.23, f32[2,48,16,128]{3,2,0,1:T(8,128)} %copy-done.2, f32[2,48,16,128]{3,2,0,1:T(8,128)S(1)} %copy_multiply_fusion, f32[2,48]{0,1:T(8,128)S(1)} %get-tuple-element.114, bf16[2,3,48,16,128]{4,3,2,1,0:T(8,128)(2,1)} %param.8), kind=kLoop, calls=%fused_computation.190 | loop fusion | flops 29491200 | bytes 12312576 | tf_op jit(solution)/shard_map/vmap()/div | solution.py:92
  200.7 1.4 copy-done.3
  202.1 2.1 fusion.152
  204.2 2.3 copy.98
  206.5 10.4 %convolution_bitcast_fusion = f32[2,48,3,64,32]{3,1,4,2,0:T(8,128)} fusion(f32[2,3,48,16,32]{2,3,4,1,0:T(8,128)} %copy.98, f32[2,16]{1,0:T(2,128)S(1)} %copy-done.5), kind=kOutput, calls=%fused_computation.197 | convolution fusion | flops 113254400 | bytes 2949248 | tf_op jit(solution)/shard_map/bcxyn,bmy->bxcmn/dot_general | solution.py:106
  216.9 9.6 %copy.99 = f32[2,48,3,64,32]{1,0,4,3,2:T(2,128)} copy(f32[2,48,3,64,32]{3,1,4,2,0:T(8,128)} %convolution_bitcast_fusion) | data formatting | bytes 4718592 | tf_op jit(solution)/shard_map/bcxyn,bmy->bxcmn/transpose | solution.py:106
  226.5 6.1 %reshape.97 = f32[96,6144]{0,1:T(8,128)S(1)} reshape(f32[2,48,3,64,32]{1,0,4,3,2:T(2,128)} %copy.99) | data formatting | bytes 4718592 | tf_op jit(solution)/shard_map/reshape | solution.py:107
  232.6 4.7 %fusion.146 = f32[96,6144]{1,0:T(8,128)} fusion(f32[96,6144]{0,1:T(8,128)S(1)} %reshape.97, f32[96]{0:T(128)S(1)} %sub.71), kind=kOutput, calls=%fused_computation.254 | convolution fusion | flops 679514112 | bytes 4718976 | tf_op jit(solution)/shard_map/dot_general | solution.py:113
  237.3 50.6 %fusion = f32[16,6144]{1,0:T(8,128)S(1)} fusion(f32[96,6144]{1,0:T(8,128)} %fusion.146), kind=kCustom, calls=%all-reduce-scatter | all-reduce-scatter fusion | flops 786433 | bytes 2753024
  287.9 4.4 %collective-permute-start = (f32[16,6144]{1,0:T(8,128)S(1)}, f32[16,6144]{1,0:T(8,128)S(1)}, u32[]{:S(2)}, u32[]{:S(2)}) collective-permute-start(f32[16,6144]{1,0:T(8,128)S(1)} %fusion), channel_id=1, source_target_pairs={{0,1},{1,2},{2,3},{3,4},{4,5},{5,6},{6,7},{8,9},{9,10},{10,11},{11... | collective-permute-start | bytes 1179656
  292.4 6.3 %collective-permute-start.1 = (f32[12,6144]{1,0:T(8,128)S(1)}, f32[12,6144]{1,0:T(8,128)S(1)}, u32[]{:S(2)}, u32[]{:S(2)}) collective-permute-start(f32[12,6144]{1,0:T(8,128)S(1)} %slice.489), channel_id=1, source_target_pairs={{0,2},{1,3},{2,4},{3,5},{4,6},{5,7},{8,10},{9,11},{10,12},{11,13},... | collective-permute-start | bytes 884744
  300.0 4.0 %collective-permute-done.1 = f32[12,6144]{1,0:T(8,128)S(1)} collective-permute-done((f32[12,6144]{1,0:T(8,128)S(1)}, f32[12,6144]{1,0:T(8,128)S(1)}, u32[]{:S(2)}, u32[]{:S(2)}) %collective-permute-start.1) | collective-permute-done | bytes 294944
  304.0 1.0 concatenate.66
  305.0 0.8 dynamic-slice_bitcast_fusion
  305.8 20.8 %all-gather.4.cloned.1.call-done = f32[4,12,6144]{2,1,0:T(8,128)} async-done(((f32[1,12,6144]{2,1,0:T(8,128)}), f32[4,12,6144]{2,1,0:T(8,128)}) %all-gather.4.cloned.1.call-update) | async-done | bytes 1179664 | tf_op jit(solution)/shard_map/all_gather | solution.py:123
  326.6 1.5 reduce_sum.9
  328.2 0.8 broadcast_multiply_fusion
  (92 shorter events, 8.3 us)
Async XLA Ops:
  7.2 3.2 copy-start.9
  7.2 3.2 copy-start.4
  7.2 2.9 copy-start.6
  7.2 3.0 copy-start.7
  7.2 319.4 %all-gather.4.cloned.1.call-start = ((), (), s32[]{:S(2)}) async-start(), calls=%async_computation | async-start | bytes 1966080 | tf_op jit(solution)/shard_map/all_gather | solution.py:123
  9.9 36.0 %copy-start.11 = (s32[4]{0:T(128)S(1)}, s32[4]{0:T(128)}, u32[]{:S(2)}) copy-start(s32[4]{0:T(128)} %constant.25.clone.1) | copy-start | bytes 52
  10.0 36.1 %copy-start.13 = (s32[5]{0:T(128)S(1)}, s32[5]{0:T(128)}, u32[]{:S(2)}) copy-start(s32[5]{0:T(128)} %constant.657) | copy-start | bytes 64
  65.7 2.0 copy-start.2
  67.7 2.2 copy-start
  135.0 1.4 copy-start.1
  200.4 1.6 copy-start.8
  200.7 1.4 copy-start.3
  204.1 2.3 copy-start.5
  226.5 6.1 %copy-start.12 = (f32[2,48]{1,0:T(2,128)S(1)}, f32[2,48]{1,0:T(2,128)}, u32[]{:S(2)}) copy-start(f32[2,48]{1,0:T(2,128)} %param.13) | copy-start | bytes 1156
  237.3 61.4 %copy-start.10 = (u32[32]{0:T(128)S(1)}, u32[32]{0:T(128)}, u32[]{:S(2)}) copy-start(u32[32]{0:T(128)} %constant.343) | copy-start | bytes 388
  287.9 16.0 %collective-permute-start = (f32[16,6144]{1,0:T(8,128)S(1)}, f32[16,6144]{1,0:T(8,128)S(1)}, u32[]{:S(2)}, u32[]{:S(2)}) collective-permute-start(f32[16,6144]{1,0:T(8,128)S(1)} %fusion), channel_id=1, source_target_pairs={{0,1},{1,2},{2,3},{3,4},{4,5},{5,6},{6,7},{8,9},{9,10},{10,11},{11... | collective-permute-start | bytes 1179656
  292.4 11.6 %collective-permute-start.1 = (f32[12,6144]{1,0:T(8,128)S(1)}, f32[12,6144]{1,0:T(8,128)S(1)}, u32[]{:S(2)}, u32[]{:S(2)}) collective-permute-start(f32[12,6144]{1,0:T(8,128)S(1)} %slice.489), channel_id=1, source_target_pairs={{0,2},{1,3},{2,4},{3,5},{4,6},{5,7},{8,10},{9,11},{10,12},{11,13},... | collective-permute-start | bytes 884744
Sparse Core Ops, SparseCore 0:
  306.0 20.5 all-gather.3
